TPU v7x, 128 devices: a whole 4x4x4 slice. The times are simulated.
128 devices in a mesh: pts: 16 (over z, y), freq: 8 (over x, core).
Axes of the slice: x: 4, y: 4, z: 4, core: 2. Of those that a mesh axis runs over, the one named last changes fastest.
Arguments:
- spectra: bfloat16 [128, 5, 4096, 128], P('freq', None, 'pts'), parts along dimension 0, may hold values from -200 to 200, as said below
- weights: float32 [4096], P('pts'), as said below
Outputs:
- mode_shapes: bfloat16 [128, 5, 4096, 128], P('freq', None, 'pts'), parts along dimension 0
There are 8 independent parts, one for each index of `freq`. A program takes and returns all parts, laid end to end along the dimension named above; an argument that names none is the same for every part. Nothing has to cross between parts.
Inputs may be any that keep to these rules, and one draw needn't show every extreme that they name: `spectra`: each row (frequency, variable, point) and each block's column pair has its own scale; the complex columns are independent. `weights`: Positive; their sum is of order one.
All inputs are finite; a program needn't handle non-finite values.
Results may differ from a plain program's by a relative error of at most 0.0054.
Values sent between devices are 32-bit elements; how exact they have to be, the bound alone decides.
No kernel may reach another device: no remote copies, remote signals or barrier semaphores. Data moves between devices by JAX's collectives and lax.ppermute only.
A program may use at most 64 MiB of HBM per device.

v0:
```python
import jax
import jax.numpy as jnp
from jax import lax
from jax.sharding import PartitionSpec as P

NS_STEPS = 10


def split_parts(products):
    half_cols = products.shape[-1] // 2
    top_left = products[:, :half_cols, :half_cols]
    top_right = products[:, :half_cols, half_cols:]
    bottom_left = products[:, half_cols:, :half_cols]
    bottom_right = products[:, half_cols:, half_cols:]
    return (top_left + bottom_right, top_right - bottom_left)


def build_cross(real_part, imag_part):
    upper_row = jnp.concatenate([real_part, imag_part], 2)
    lower_row = jnp.concatenate([-imag_part, real_part], 2)
    return jnp.concatenate([upper_row, lower_row], 1)


def upper_of(cross_gram):
    order = cross_gram.shape[-1]
    places = jnp.arange(order)

    def eliminate(column, carry):
        working, factor = carry
        picker = (places == column).astype(jnp.float32)
        below = (places >= column).astype(jnp.float32)
        current = jnp.sum(working * picker[None, None, :], axis=2) * below[None, :]
        pivot = jnp.sqrt(jnp.sum(current * picker[None, :], axis=1))
        scaled = current / pivot[:, None]
        factor = factor + scaled[:, None, :] * picker[None, :, None]
        working = working - scaled[:, :, None] * scaled[:, None, :]
        return (working, factor)

    start = (cross_gram, jnp.zeros_like(cross_gram))
    working, factor = lax.fori_loop(0, order, eliminate, start)
    return factor


def solve_upper(upper_factor, right_side):
    order = upper_factor.shape[-1]
    places = jnp.arange(order)

    def back_step(count, solved):
        row = order - 1 - count
        picker = (places == row).astype(jnp.float32)
        factor_row = jnp.sum(upper_factor * picker[None, :, None], axis=1)
        side_row = jnp.sum(right_side * picker[None, :, None], axis=1)
        pivot = jnp.sum(factor_row * picker[None, :], axis=1)
        known = jnp.einsum("fj,fjk->fk", factor_row, solved, precision=lax.Precision.HIGHEST)
        value = (side_row - known) / pivot[:, None]
        return solved + picker[None, :, None] * value[:, None, :]

    return lax.fori_loop(0, order, back_step, jnp.zeros_like(right_side))


def gram_of(upper_factor):
    return jnp.einsum("fki,fkj->fij", upper_factor, upper_factor, precision=lax.Precision.HIGHEST)


def local(spectra, weights):
    freq_count, var_count, point_count, col_count = spectra.shape
    root_weights = jnp.sqrt(weights)
    weighted = (root_weights[None, None, :, None] * spectra.astype(jnp.float32)).astype(
        jnp.bfloat16
    )
    flat_rows = weighted.reshape(freq_count, var_count * point_count, col_count)
    products = jnp.einsum("frc,frd->fcd", flat_rows, flat_rows, preferred_element_type=jnp.float32)
    real_part, imag_part = split_parts(products)
    cross_gram = build_cross(real_part, imag_part)
    summed = lax.psum(cross_gram, "pts")
    upper_factor = upper_of(summed)
    frob_norm = jnp.sqrt(jnp.sum(upper_factor * upper_factor, axis=(1, 2)))
    polar = upper_factor / frob_norm[:, None, None]
    for sweep in range(NS_STEPS):
        inner_gram = gram_of(polar)
        polar = 1.5 * polar - 0.5 * jnp.einsum(
            "fij,fjk->fik", polar, inner_gram, precision=lax.Precision.HIGHEST
        )
    mapping = solve_upper(upper_factor, polar).astype(jnp.bfloat16)
    shapes = jnp.einsum("fvpc,fcd->fvpd", spectra, mapping, preferred_element_type=jnp.float32)
    return shapes.astype(jnp.bfloat16)


def solution(mesh):
    in_specs = (P("freq", None, "pts", None), P("pts"))
    out_specs = P("freq", None, "pts", None)
    return jax.shard_map(local, mesh=mesh, in_specs=in_specs, out_specs=out_specs, check_vma=False)
```

profile of v0, /device:TPU:0, one launch (start us, length us, event | category | flops | bytes accessed | tf_op | source)
XLA Modules:
  0.0 935.5 jit_solution(8490604428545319796)
XLA Ops:
  7.2 4.0 multiply_convert_fusion
  14.6 90.1 %all-reduce.2.cloned.1.call-done = f32[16,128,128]{2,1,0:T(8,128)} async-done(((f32[16,128,128]{2,1,0:T(8,128)}), f32[16,128,128]{2,1,0:T(8,128)}) %all-reduce.2.cloned.1.call-update) | async-done | bytes 1048592 | tf_op jit(solution)/shard_map/psum | solution.py:75
  104.7 568.0 %while.32 = (s32[]{:T(128)}, f32[16,128,128]{2,1,0:T(8,128)}, f32[16,128,128]{2,1,0:T(8,128)S(1)}, s32[]{:T(128)}, s32[]{:T(128)}) while((s32[]{:T(128)}, f32[16,128,128]{2,1,0:T(8,128)}, f32[16,128,128]{2,1,0:T(8,128)S(1)}, s32[]{:T(128)}, s32[]{:T(128)}) %tuple.73), condition=%wide.region_4.0_spmd.clone.clone, body=%wide.region_1.0_spmd.clone.clone.sunk | while | flops 1843699 | bytes 5287763 | solution.py:40
  106.5 2.7 select_add_fusion.2
  110.9 2.7 select_add_fusion.2
  115.3 2.7 select_add_fusion.2
  124.2 2.7 select_add_fusion.2
  133.1 2.7 select_add_fusion.2
  137.5 2.7 select_add_fusion.2
  141.9 2.7 select_add_fusion.2
  146.4 2.7 select_add_fusion.2
  150.8 2.7 select_add_fusion.2
  155.2 2.7 select_add_fusion.2
  159.7 2.7 select_add_fusion.2
  164.1 2.7 select_add_fusion.2
  168.5 2.7 select_add_fusion.2
  173.0 2.7 select_add_fusion.2
  177.4 2.7 select_add_fusion.2
  181.8 2.7 select_add_fusion.2
  186.3 2.7 select_add_fusion.2
  190.7 2.7 select_add_fusion.2
  195.1 2.7 select_add_fusion.2
  199.6 2.7 select_add_fusion.2
  208.4 2.7 select_add_fusion.2
  217.3 2.7 select_add_fusion.2
  221.7 2.7 select_add_fusion.2
  226.2 2.7 select_add_fusion.2
  230.6 2.7 select_add_fusion.2
  235.0 2.7 select_add_fusion.2
  239.5 2.7 select_add_fusion.2
  243.9 2.7 select_add_fusion.2
  248.3 2.7 select_add_fusion.2
  252.8 2.7 select_add_fusion.2
  257.2 2.7 select_add_fusion.2
  261.7 2.7 select_add_fusion.2
  266.1 2.7 select_add_fusion.2
  270.5 2.7 select_add_fusion.2
  275.0 2.7 select_add_fusion.2
  279.4 2.7 select_add_fusion.2
  283.8 2.7 select_add_fusion.2
  292.7 2.7 select_add_fusion.2
  301.6 2.7 select_add_fusion.2
  306.0 2.7 select_add_fusion.2
  310.4 2.7 select_add_fusion.2
  314.9 2.7 select_add_fusion.2
  705.7 208.5 %while.31 = (s32[]{:T(128)}, f32[16,128,128]{2,1,0:T(8,128)S(1)}, f32[16,128,128]{2,1,0:T(8,128)S(1)}, f32[16,128,128]{2,1,0:T(8,128)S(1)}, s32[]{:T(128)}, /*index=5*/s32[]{:T(128)}, s32[]{:T(128)}) while((s32[]{:T(128)}, f32[16,128,128]{2,1,0:T(8,128)S(1)}, f32[16,128,128]{2,1,0:T(8,128)S(1)}, f32[16,128,128]{2,1,0:T(8,128)S(1)}, ...), condition=%wide.region_10.0_spmd.clone, body=%wide.region_6.0_spmd.clone.sunk | while | flops 5247220 | bytes 5318896 | solution.py:58
  914.2 6.4 convert_bitcast_fusion
  920.6 7.8 copy.8
  (1524 shorter events, 695.3 us)
Async XLA Ops:
  6.5 98.1 %all-reduce.2.cloned.1.call-start = ((), (), s32[]{:S(2)}) async-start(), calls=%async_computation | async-start | bytes 2097152 | tf_op jit(solution)/shard_map/psum | solution.py:75
Sparse Core Ops, SparseCore 0:
  14.7 89.9 all-reduce.1
where the time goes:
time: 950 us; the launch traced here: 936 us
  other arithmetic  655 us (69%)
  matrix products  160 us (17%)
  waiting for transfers between devices  90.1 us (9%)
  between operations  13.8 us (1%)
  local copies, waits for them, and re-layouts  9.6 us (1%)
    add x128, other arithmetic, eliminate(): factor = factor + scaled[:, None, :] * picker[None, :, None]  340 us
    reduce_sum x128, other arithmetic, eliminate(): current = jnp.sum(working * picker[None, None, :], axis=2) * below[None, :]  200 us
    dot_general x128, matrix products, back_step(): jnp.einsum('fj,fjk->fk', factor_row, solved, precision=lax.Precision.HIGH...  120 us
    psum x1, waiting for transfers between devices, local(): summed = lax.psum(cross_gram, 'pts')  90.1 us
    reduce_sum x128, other arithmetic, back_step(): factor_row = jnp.sum(upper_factor * picker[None, :, None], axis=1)  33.5 us
    add x128, other arithmetic, back_step(): return solved + picker[None, :, None] * value[:, None, :]  25.6 us
    dot_general x10, matrix products, gram_of(): jnp.einsum('fki,fkj->fij', upper_factor, upper_factor, precision=lax.Prec...  19.4 us
  transfers between devices with their start and end apart: 1, of which 1 were waited for; matrix products, arithmetic and copies ran while one was open for 0% of the time, Pallas kernels for 0%

commit v1 on v0

--- a/solution.py
+++ b/solution.py
@@ -72,7 +72,10 @@
     products = jnp.einsum("frc,frd->fcd", flat_rows, flat_rows, preferred_element_type=jnp.float32)
     real_part, imag_part = split_parts(products)
     cross_gram = build_cross(real_part, imag_part)
-    summed = lax.psum(cross_gram, "pts")
+    size, summed = (lax.axis_size("pts"), cross_gram)
+    for far in [1 << k for k in range(size.bit_length() - 1)]:
+        pairs = [(i, i ^ far) for i in range(size)]
+        summed = summed + lax.ppermute(summed, "pts", pairs)
     upper_factor = upper_of(summed)
     frob_norm = jnp.sqrt(jnp.sum(upper_factor * upper_factor, axis=(1, 2)))
     polar = upper_factor / frob_norm[:, None, None]

time: 950 us -> 530 us (0.56); the launches traced: 936 us -> 525 us
  other arithmetic: 655 us -> 244 us
  between operations: 13.8 us -> 0.44 us
  starting transfers between devices: 0.01 us -> 11.4 us
    add x128, other arithmetic: 340 us -> 84.3 us  [eliminate(): factor = factor + scaled[:, None, :] * picker[None, :, None]]
    reduce_sum x128, other arithmetic: 200 us -> 44 us  [eliminate(): current = jnp.sum(working * picker[None, None, :], axis=2) * below[None, :]]
    psum x1 -> x0, waiting for transfers between devices: 90.1 us -> none  [local(): summed = lax.psum(cross_gram, 'pts')]
    ppermute x0 -> x4, waiting for transfers between devices: none -> 88.5 us  [local(): summed = summed + lax.ppermute(summed, 'pts', pairs)]
    ppermute x0 -> x4, starting transfers between devices: none -> 11.4 us  [local(): summed = summed + lax.ppermute(summed, 'pts', pairs)]
  transfers between devices with their start and end apart: 1 -> 4, of which waited for: 1 -> 4; matrix products, arithmetic and copies ran while one was open for 0% -> 0% of each run, Pallas kernels for 0% -> 0%
where the time goes in v1:
time: 530 us; the launch traced here: 525 us
  other arithmetic  244 us (46%)
  matrix products  160 us (30%)
  waiting for transfers between devices  88.5 us (17%)
  starting transfers between devices  11.4 us (2%)
  loops' own time  10.6 us (2%)
  local copies, waits for them, and re-layouts  9.61 us (2%)
    dot_general x128, matrix products, back_step(): jnp.einsum('fj,fjk->fk', factor_row, solved, precision=lax.Precision.HIGH...  120 us
    ppermute x4, waiting for transfers between devices, local(): summed = summed + lax.ppermute(summed, 'pts', pairs)  88.5 us
    add x128, other arithmetic, eliminate(): factor = factor + scaled[:, None, :] * picker[None, :, None]  84.3 us
    reduce_sum x128, other arithmetic, eliminate(): current = jnp.sum(working * picker[None, None, :], axis=2) * below[None, :]  44 us
    reduce_sum x128, other arithmetic, back_step(): factor_row = jnp.sum(upper_factor * picker[None, :, None], axis=1)  33.5 us
    add x128, other arithmetic, back_step(): return solved + picker[None, :, None] * value[:, None, :]  25.4 us
    dot_general x10, matrix products, gram_of(): jnp.einsum('fki,fkj->fij', upper_factor, upper_factor, precision=lax.Prec...  19.4 us
    reduce_sum x128, other arithmetic, eliminate(): pivot = jnp.sqrt(jnp.sum(current * picker[None, :], axis=1))  14.6 us
  transfers between devices with their start and end apart: 4, of which 4 were waited for; matrix products, arithmetic and copies ran while one was open for 0% of the time, Pallas kernels for 0%

profile of v1, /device:TPU:0, one launch (start us, length us, event | category | flops | bytes accessed | tf_op | source)
XLA Modules:
  0.0 525.3 jit_solution(7766796865143851328)
XLA Ops:
  0.7 4.0 multiply_convert_fusion
  4.7 1.6 fusion.23
  7.1 1.8 collective-permute-start
  8.8 23.2 %collective-permute-done = f32[16,128,128]{2,1,0:T(8,128)S(1)} collective-permute-done((f32[16,128,128]{2,1,0:T(8,128)S(1)}, f32[16,128,128]{2,1,0:T(8,128)S(1)}, u32[]{:S(2)}, u32[]{:S(2)}) %collective-permute-start) | collective-permute-done | bytes 1048608 | tf_op jit(solution)/shard_map/ppermute | solution.py:78
  32.3 3.4 collective-permute-start.1
  35.8 22.3 %collective-permute-done.1 = f32[16,128,128]{2,1,0:T(8,128)S(1)} collective-permute-done((f32[16,128,128]{2,1,0:T(8,128)S(1)}, f32[16,128,128]{2,1,0:T(8,128)S(1)}, u32[]{:S(2)}, u32[]{:S(2)}) %collective-permute-start.1) | collective-permute-done | bytes 1048608 | tf_op jit(solution)/shard_map/ppermute | solution.py:78
  58.2 2.0 collective-permute-start.2
  60.3 21.4 %collective-permute-done.2 = f32[16,128,128]{2,1,0:T(8,128)S(1)} collective-permute-done((f32[16,128,128]{2,1,0:T(8,128)S(1)}, f32[16,128,128]{2,1,0:T(8,128)S(1)}, u32[]{:S(2)}, u32[]{:S(2)}) %collective-permute-start.2) | collective-permute-done | bytes 1048608 | tf_op jit(solution)/shard_map/ppermute | solution.py:78
  81.8 4.2 collective-permute-start.3
  86.0 21.6 %collective-permute-done.3 = f32[16,128,128]{2,1,0:T(8,128)} collective-permute-done((f32[16,128,128]{2,1,0:T(8,128)S(1)}, f32[16,128,128]{2,1,0:T(8,128)}, u32[]{:S(2)}, u32[]{:S(2)}) %collective-permute-start.3) | collective-permute-done | bytes 1048608 | tf_op jit(solution)/shard_map/ppermute | solution.py:78
  107.6 1.7 add.65
  109.2 160.3 %while.32 = (s32[]{:T(128)}, f32[16,128,128]{2,1,0:T(8,128)S(1)}, f32[16,128,128]{2,1,0:T(8,128)S(1)}, s32[]{:T(128)}, s32[]{:T(128)}) while((s32[]{:T(128)}, f32[16,128,128]{2,1,0:T(8,128)S(1)}, f32[16,128,128]{2,1,0:T(8,128)S(1)}, s32[]{:T(128)}, s32[]{:T(128)}) %tuple.73), condition=%wide.region_3.0_spmd.clone.clone, body=%wide.region_0.0_spmd.clone.clone.sunk | while | flops 1843699 | bytes 5287763 | solution.py:40
  269.7 1.9 fusion.21
  271.7 1.4 fusion.18
  273.1 1.9 fusion.24
  275.0 1.3 fusion.17
  276.3 1.9 fusion.25
  278.2 1.3 fusion.16
  279.5 1.9 fusion.26
  281.5 1.5 fusion.15
  282.9 1.9 fusion.27
  284.9 1.3 fusion.14
  286.2 1.9 fusion.28
  288.1 1.3 fusion.13
  289.4 1.9 fusion.29
  291.3 1.3 fusion.12
  292.6 2.1 fusion.30
  294.8 1.3 fusion.11
  296.1 1.9 fusion.31
  298.0 1.3 fusion.10
  299.3 1.9 fusion.32
  301.2 1.3 fusion.9
  302.5 208.3 %while.31 = (s32[]{:T(128)}, f32[16,128,128]{2,1,0:T(8,128)S(1)}, f32[16,128,128]{2,1,0:T(8,128)S(1)}, f32[16,128,128]{2,1,0:T(8,128)S(1)}, s32[]{:T(128)}, /*index=5*/s32[]{:T(128)}, s32[]{:T(128)}) while((s32[]{:T(128)}, f32[16,128,128]{2,1,0:T(8,128)S(1)}, f32[16,128,128]{2,1,0:T(8,128)S(1)}, f32[16,128,128]{2,1,0:T(8,128)S(1)}, ...), condition=%wide.region_9.0_spmd.clone, body=%wide.region_5.0_spmd.clone.sunk | while | flops 5247220 | bytes 5318896 | solution.py:58
  303.0 0.9 fusion.80
  306.2 0.9 fusion.80
  309.5 0.9 fusion.80
  311.1 0.9 fusion.80
  314.3 0.9 fusion.80
  317.6 0.9 fusion.80
  322.5 0.9 fusion.80
  325.7 0.9 fusion.80
  329.0 0.9 fusion.80
  330.6 0.9 fusion.80
  333.9 0.9 fusion.80
  337.1 0.9 fusion.80
  340.4 0.9 fusion.80
  510.9 6.4 %convert_bitcast_fusion = bf16[16,5,256,128]{2,3,1,0:T(8,128)(2,1)} fusion(bf16[16,5,256,128]{3,2,1,0:T(8,128)(2,1)} %param.6, f32[16,128,128]{2,1,0:T(8,128)S(1)} %get-tuple-element.182), kind=kOutput, calls=%fused_computation.21 | convolution fusion | flops 673972224 | bytes 11534336 | tf_op jit(solution)/shard_map/fvpc,fcd->fvpd/dot_general | solution.py:88
  517.2 7.8 %copy.8 = bf16[16,5,256,128]{3,2,1,0:T(8,128)(2,1)} copy(bf16[16,5,256,128]{2,3,1,0:T(8,128)(2,1)} %convert_bitcast_fusion) | data formatting | bytes 10485760 | tf_op jit(solution)/shard_map/convert_element_type | solution.py:89
  (1535 shorter events, 348.0 us)
Async XLA Ops:
  7.1 24.9 %collective-permute-start = (f32[16,128,128]{2,1,0:T(8,128)S(1)}, f32[16,128,128]{2,1,0:T(8,128)S(1)}, u32[]{:S(2)}, u32[]{:S(2)}) collective-permute-start(f32[16,128,128]{2,1,0:T(8,128)S(1)} %maximum_maximum_fusion), channel_id=1, source_target_pairs={{0,8},{8,0},{16,24},{24,16},{32,40},{40,32},{48,56},{56,48},{64,72... | collective-permute-start | bytes 3145736 | tf_op jit(solution)/shard_map/ppermute | solution.py:78
  32.3 25.7 %collective-permute-start.1 = (f32[16,128,128]{2,1,0:T(8,128)S(1)}, f32[16,128,128]{2,1,0:T(8,128)S(1)}, u32[]{:S(2)}, u32[]{:S(2)}) collective-permute-start(f32[16,128,128]{2,1,0:T(8,128)S(1)} %fusion.74), channel_id=1, source_target_pairs={{0,16},{8,24},{16,0},{24,8},{32,48},{40,56},{48,32},{56,40},{64,80... | collective-permute-start | bytes 3145736 | tf_op jit(solution)/shard_map/ppermute | solution.py:78
  58.2 23.5 %collective-permute-start.2 = (f32[16,128,128]{2,1,0:T(8,128)S(1)}, f32[16,128,128]{2,1,0:T(8,128)S(1)}, u32[]{:S(2)}, u32[]{:S(2)}) collective-permute-start(f32[16,128,128]{2,1,0:T(8,128)S(1)} %add.63), channel_id=1, source_target_pairs={{0,32},{8,40},{16,48},{24,56},{32,0},{40,8},{48,16},{56,24},{64,96... | collective-permute-start | bytes 3145736 | tf_op jit(solution)/shard_map/ppermute | solution.py:78
  81.8 4.2 copy-start
  81.8 25.7 %collective-permute-start.3 = (f32[16,128,128]{2,1,0:T(8,128)S(1)}, f32[16,128,128]{2,1,0:T(8,128)}, u32[]{:S(2)}, u32[]{:S(2)}) collective-permute-start(f32[16,128,128]{2,1,0:T(8,128)S(1)} %add.64), channel_id=1, source_target_pairs={{0,64},{8,72},{16,80},{24,88},{32,96},{40,104},{48,112},{56,120},{... | collective-permute-start | bytes 3145736 | tf_op jit(solution)/shard_map/ppermute | solution.py:78
